TPU v7x, 32 devices: a whole 2x2x4 slice. The times are simulated.
32 devices in a mesh: row: 4 (over z), col: 2 (over x), rep: 4 (over y, core).
Axes of the slice: x: 2, y: 2, z: 4, core: 2. Of those that a mesh axis runs over, the one named last changes fastest.
Arguments:
- density: bfloat16 [1536, 1536], P('row', 'col'), as said below
- keep_square: int32 [12, 12], P('row', 'col'), may hold values 0 or 1
- keep_cube: int32 [12, 12], P('row', 'col'), may hold values 0 or 1
Outputs:
- purified: float32 [1536, 1536], P(('row', 'rep'), 'col')
Inputs may be any that keep to these rules, and one draw needn't show every extreme that they name: density is symmetric; its 128 x 128 diagonal blocks are always occupied, any other block may be zero or occupied at any distance from the diagonal.
All inputs are finite; a program needn't handle non-finite values. No bound on the sum of `keep_square` or of `keep_cube` on one device may be relied on, other than what follows from the above.
Results may differ from a plain program's by a relative error of at most 0.002.
Values may be sent and summed in bfloat16 or wider, within the bound.
A program may use at most 64 MiB of HBM per device.

v0:
```python
import jax
import jax.numpy as jnp
from jax import lax
from jax.sharding import PartitionSpec as P

BLK = 128


def broadcast(array, axis, root):
    mine = lax.axis_index(axis) == root
    return lax.psum(jnp.where(mine, array, jnp.zeros_like(array)), axis)


def widen(mask, tile_rows, tile_cols):
    blocks = jnp.broadcast_to(
        mask.astype(jnp.float32)[:, None, :, None], (mask.shape[0], BLK, mask.shape[1], BLK)
    )
    return blocks.reshape(tile_rows, tile_cols)


def left_piece(tile, piece_index):
    height = tile.shape[0]
    per_tile = tile.shape[1] // height
    column = lax.dynamic_slice_in_dim(tile, piece_index % per_tile * height, height, 1)
    return broadcast(column, "col", piece_index // per_tile)


def right_piece(density, piece_index):
    return broadcast(density, "row", piece_index)


def local(density, keep_square, keep_cube):
    tile_rows, tile_cols = density.shape
    rep_count = lax.axis_size("rep")
    row_count = lax.axis_size("row")
    rep_index = lax.axis_index("rep")
    sections = row_count // rep_count
    indices = [position * rep_count + rep_index for position in range(sections)]
    square_total = jnp.zeros((tile_rows, tile_cols), jnp.float32)
    for piece_index in indices:
        right_panel = right_piece(density, piece_index)
        square_total = square_total + jnp.dot(
            left_piece(density, piece_index), right_panel, preferred_element_type=jnp.float32
        )
    square_total = square_total * widen(keep_square, tile_rows, tile_cols)
    square_own = lax.psum_scatter(square_total, "rep", scatter_dimension=0, tiled=True)
    square_low = lax.all_gather(square_own.astype(jnp.bfloat16), "rep", axis=0, tiled=True)
    cube_total = jnp.zeros((tile_rows, tile_cols), jnp.float32)
    for number, piece_index in enumerate(indices):
        right_panel = right_piece(density, piece_index)
        cube_total = cube_total + jnp.dot(
            left_piece(square_low, piece_index), right_panel, preferred_element_type=jnp.float32
        )
    cube_total = cube_total * widen(keep_cube, tile_rows, tile_cols)
    cube_own = lax.psum_scatter(cube_total, "rep", scatter_dimension=0, tiled=True)
    return 3.0 * square_own - 2.0 * cube_own


def solution(mesh):
    return jax.shard_map(
        local,
        mesh=mesh,
        in_specs=(P("row", "col"), P("row", "col"), P("row", "col")),
        out_specs=P(("row", "rep"), "col"),
        check_vma=False,
    )
```

profile of v0, /device:TPU:0, one launch (start us, length us, event | category | flops | bytes accessed | tf_op | source)
XLA Modules:
  0.0 175.6 jit_solution(14447856597460182150)
XLA Ops:
  6.5 0.0 all-reduce.4.cloned.1.call-start
  6.5 1.8 %dynamic-slice_select_fusion.1 = bf16[384,384]{1,0:T(8,128)(2,1)} fusion(bf16[384,768]{1,0:T(8,128)(2,1)} %param.3, s32[]{:T(128)S(6)} %select_n.43, pred[]{:T(512)S(6)} %eq.11), kind=kLoop, calls=%fused_computation.5 | loop fusion | flops 147456 | bytes 589829 | tf_op jit(solution)/shard_map/jit(_where)/select_n | solution.py:11
  8.3 0.0 all-reduce.4.cloned.1.call-update
  8.4 0.0 all-reduce.6.cloned.1.call-start
  8.4 0.0 copy-done.1
  8.4 0.9 broadcast_select_fusion
  9.3 0.0 all-reduce.6.cloned.1.call-update
  9.3 0.0 reduce-scatter.3.cloned.1.call-start
  9.4 0.0 copy-done.5
  9.4 26.7 %all-reduce.4.cloned.1.call-done = bf16[384,384]{1,0:T(8,128)(2,1)} async-done(((bf16[384,384]{1,0:T(8,128)(2,1)}), bf16[384,384]{1,0:T(8,128)(2,1)}) %all-reduce.4.cloned.1.call-update) | async-done | bytes 294928 | tf_op jit(solution)/shard_map/psum | solution.py:11
  36.1 42.0 %all-reduce.6.cloned.1.call-done = bf16[384,768]{1,0:T(8,128)(2,1)} async-done(((bf16[384,768]{1,0:T(8,128)(2,1)}), bf16[384,768]{1,0:T(8,128)(2,1)}) %all-reduce.6.cloned.1.call-update) | async-done | bytes 589840 | tf_op jit(solution)/shard_map/psum | solution.py:11
  78.1 0.2 broadcast_in_dim.4
  78.3 0.0 copy-done.3
  78.3 0.9 copy-done
  79.2 1.5 convolution_multiply_fusion.1
  80.7 0.0 reduce-scatter.3.cloned.1.call-update
  80.7 0.0 copy-start.6
  80.7 0.0 all-reduce.8.cloned.1.call-start
  80.8 25.2 %reduce-scatter.3.cloned.1.call-done = f32[96,768]{1,0:T(8,128)} async-done(((f32[384,768]{1,0:T(8,128)}), f32[96,768]{1,0:T(8,128)}) %reduce-scatter.3.cloned.1.call-update) | async-done | bytes 294928 | tf_op jit(solution)/shard_map/reduce_scatter | solution.py:46
  105.9 1.0 convert_element_type.10
  106.9 6.9 %all_gather.3 = bf16[384,768]{1,0:T(8,128)(2,1)S(1)} all-gather(bf16[96,768]{1,0:T(8,128)(2,1)S(1)} %convert_element_type.10), channel_id=1, replica_groups=mesh['row'=4,'col'=2,'rep'=4] {'rep'}, dimensions={0}, use_global_device_ids=true | all-gather | bytes 737280 | tf_op jit(solution)/shard_map/all_gather | solution.py:47
  113.9 0.8 dynamic-slice_select_fusion
  114.6 0.0 all-reduce.8.cloned.1.call-update
  114.7 0.0 reduce-scatter.5.cloned.1.call-start
  114.7 0.0 copy-done.6
  114.7 24.3 %all-reduce.8.cloned.1.call-done = bf16[384,384]{1,0:T(8,128)(2,1)} async-done(((bf16[384,384]{1,0:T(8,128)(2,1)}), bf16[384,384]{1,0:T(8,128)(2,1)}) %all-reduce.8.cloned.1.call-update) | async-done | bytes 294928 | tf_op jit(solution)/shard_map/psum | solution.py:11
  139.1 0.2 broadcast_in_dim.5
  139.2 0.8 copy-done.4
  140.0 1.5 convolution_multiply_fusion
  141.5 0.0 reduce-scatter.5.cloned.1.call-update
  141.5 25.8 %reduce-scatter.5.cloned.1.call-done = f32[96,768]{1,0:T(8,128)} async-done(((f32[384,768]{1,0:T(8,128)}), f32[96,768]{1,0:T(8,128)}) %reduce-scatter.5.cloned.1.call-update) | async-done | bytes 294928 | tf_op jit(solution)/shard_map/reduce_scatter | solution.py:55
  167.3 1.7 multiply_subtract_fusion
  (9 shorter events, 0.0 us)
Async XLA Ops:
  6.5 1.9 %copy-start.1 = (bf16[384,768]{1,0:T(8,128)(2,1)S(1)}, bf16[384,768]{1,0:T(8,128)(2,1)}, u32[]{:S(2)}) copy-start(bf16[384,768]{1,0:T(8,128)(2,1)} %param.3) | copy-start | bytes 1769476
  6.5 29.5 %all-reduce.4.cloned.1.call-start = ((), (), s32[]{:S(2)}) async-start(), calls=%async_computation.2 | async-start | bytes 589824 | tf_op jit(solution)/shard_map/psum | solution.py:11
  8.3 1.0 copy-start.5
  8.4 69.7 %all-reduce.6.cloned.1.call-start = ((), (), s32[]{:S(2)}) async-start(), calls=%async_computation.3 | async-start | bytes 1179648 | tf_op jit(solution)/shard_map/psum | solution.py:11
  9.3 96.6 %reduce-scatter.3.cloned.1.call-start = ((), (), s32[]{:S(2)}) async-start(), calls=%async_computation.4 | async-start | bytes 1474560 | tf_op jit(solution)/shard_map/reduce_scatter | solution.py:46
  36.1 42.2 %copy-start.3 = (bf16[384,384]{1,0:T(8,128)(2,1)S(1)}, bf16[384,384]{1,0:T(8,128)(2,1)}, u32[]{:S(2)}) copy-start(bf16[384,384]{1,0:T(8,128)(2,1)} %all-reduce.4.cloned.1.call-done) | copy-start | bytes 884740
  78.1 1.1 copy-start
  80.7 34.0 %copy-start.6 = (s32[3,6]{1,0:T(4,128)S(1)}, s32[3,6]{1,0:T(4,128)}, u32[]{:S(2)}) copy-start(s32[3,6]{1,0:T(4,128)} %param.5) | copy-start | bytes 220
  80.7 58.4 %all-reduce.8.cloned.1.call-start = ((), (), s32[]{:S(2)}) async-start(), calls=%async_computation.5 | async-start | bytes 589824 | tf_op jit(solution)/shard_map/psum | solution.py:11
  114.7 52.7 %reduce-scatter.5.cloned.1.call-start = ((), (), s32[]{:S(2)}) async-start(), calls=%async_computation.6 | async-start | bytes 1474560 | tf_op jit(solution)/shard_map/reduce_scatter | solution.py:55
  139.1 1.0 copy-start.4
  141.5 25.8 %copy-start.2 = (f32[96,768]{1,0:T(8,128)S(1)}, f32[96,768]{1,0:T(8,128)}, u32[]{:S(2)}) copy-start(f32[96,768]{1,0:T(8,128)} %reduce-scatter.3.cloned.1.call-done) | copy-start | bytes 884740
Sparse Core Ops, SparseCore 0:
  9.6 26.4 all-reduce.3
  38.4 39.6 all-reduce.5
  80.8 25.0 reduce-scatter.2
  114.8 24.2 all-reduce.7
  141.7 25.6 reduce-scatter.4
where the time goes:
time: 176 us
  waiting for transfers between devices  144 us (82%)
  between operations  13.2 us (8%)
  blocking collectives  6.95 us (4%)
  other arithmetic  6.12 us (3%)
  matrix products  3 us (2%)
  local copies, waits for them, and re-layouts  2.03 us (1%)
    psum x3, waiting for transfers between devices, broadcast(): return lax.psum(jnp.where(mine, array, jnp.zeros_like(array)), axis)  93 us
    reduce_scatter x1, waiting for transfers between devices, local(): lax.psum_scatter(cube_total, 'rep', scatter_dimension=0, tiled=True)  25.8 us
    reduce_scatter x1, waiting for transfers between devices, local(): lax.psum_scatter(square_total, 'rep', scatter_dimension=0, tiled=True)  25.2 us
    all_gather x1, blocking collectives, local(): lax.all_gather(square_own.astype(jnp.bfloat16), 'rep', axis=0, tiled=True)  6.95 us
  transfers between devices with their start and end apart: 5, of which 5 were waited for; matrix products, arithmetic and copies ran while one was open for 0% of the time, Pallas kernels for 0%

commit v1 on v0

--- a/solution.py
+++ b/solution.py
@@ -8,7 +8,7 @@
 
 def broadcast(array, axis, root):
     mine = lax.axis_index(axis) == root
-    return lax.psum(jnp.where(mine, array, jnp.zeros_like(array)), axis)
+    return jnp.sum(lax.all_gather(jnp.where(mine, array, jnp.zeros_like(array)), axis), axis=0)
 
 
 def widen(mask, tile_rows, tile_cols):

time: 176 us -> 145 us (0.82)
  waiting for transfers between devices: 144 us -> 93.1 us
  blocking collectives: 6.95 us -> 26.6 us
    psum x3 -> x0, waiting for transfers between devices: 93 us -> none  [broadcast(): return lax.psum(jnp.where(mine, array, jnp.zeros_like(array)), axis)]
    all_gather x0 -> x1, waiting for transfers between devices: none -> 42.9 us  [broadcast(): lax.all_gather(jnp.where(mine, array, jnp.zeros_like(array)), axis)]
    all_gather x0 -> x2, blocking collectives: none -> 19.7 us  [broadcast(): lax.all_gather(jnp.where(mine, array, jnp.zeros_like(array)), axis)]
    reduce_sum x0 -> x3, other arithmetic: none -> 2.65 us  [broadcast(): jnp.sum(lax.all_gather(jnp.where(mine, array, jnp.zeros_like(array)), axi...]
  transfers between devices with their start and end apart: 5 -> 3, of which waited for: 5 -> 3; matrix products, arithmetic and copies ran while one was open for 0% -> 0% of each run, Pallas kernels for 0% -> 0%
where the time goes in v1:
time: 145 us; the launch traced here: 144 us
  waiting for transfers between devices  93.1 us (64%)
  blocking collectives  26.6 us (18%)
  between operations  13.2 us (9%)
  other arithmetic  7.47 us (5%)
  matrix products  2.98 us (2%)
    all_gather x1, waiting for transfers between devices, broadcast(): lax.all_gather(jnp.where(mine, array, jnp.zeros_like(array)), axis)  42.9 us
    reduce_scatter x1, waiting for transfers between devices, local(): lax.psum_scatter(cube_total, 'rep', scatter_dimension=0, tiled=True)  26.3 us
    reduce_scatter x1, waiting for transfers between devices, local(): lax.psum_scatter(square_total, 'rep', scatter_dimension=0, tiled=True)  23.9 us
    all_gather x2, blocking collectives, broadcast(): lax.all_gather(jnp.where(mine, array, jnp.zeros_like(array)), axis)  19.7 us
    all_gather x1, blocking collectives, local(): lax.all_gather(square_own.astype(jnp.bfloat16), 'rep', axis=0, tiled=True)  6.96 us
  transfers between devices with their start and end apart: 3, of which 3 were waited for; matrix products, arithmetic and copies ran while one was open for 0% of the time, Pallas kernels for 0%

profile of v1, /device:TPU:0, one launch (start us, length us, event | category | flops | bytes accessed | tf_op | source)
XLA Modules:
  0.0 144.5 jit_solution(9834058554268184638)
XLA Ops:
  6.5 0.0 copy-start
  6.5 0.0 copy-start.2
  6.5 0.0 all-gather.5.cloned.1.call-start
  6.5 2.0 %broadcast_select_fusion = bf16[384,768]{1,0:T(8,128)(2,1)} fusion(bf16[384,768]{1,0:T(8,128)(2,1)} %param.3, pred[]{:T(512)S(6)} %eq.12), kind=kLoop, calls=%fused_computation.2 | loop fusion | flops 294912 | bytes 1179649 | tf_op jit(solution)/shard_map/jit(_where)/select_n | solution.py:11
  8.5 0.0 all-gather.5.cloned.1.call-update
  8.6 0.0 reduce-scatter.3.cloned.1.call-start
  8.6 0.0 copy-done.2
  8.7 0.0 copy-done
  8.7 0.1 dynamic-slice_select_fusion.1
  8.8 9.8 %all-gather = bf16[768,384]{1,0:T(8,128)(2,1)S(1)} all-gather(bf16[384,384]{1,0:T(8,128)(2,1)S(1)} %dynamic-slice_select_fusion.1), channel_id=2, replica_groups=mesh['row'=4,'col'=2,'rep'=4] {'col'}, dimensions={0}, use_global_device_ids=true | all-gather | bytes 884736 | tf_op jit(solution)/shard_map/all_gather | solution.py:11
  18.5 0.2 reduce_sum.40
  18.7 42.9 %all-gather.5.cloned.1.call-done = bf16[1536,768]{1,0:T(8,128)(2,1)} async-done(((bf16[384,768]{1,0:T(8,128)(2,1)}), bf16[1536,768]{1,0:T(8,128)(2,1)}) %all-gather.5.cloned.1.call-update) | async-done | bytes 2359312 | tf_op jit(solution)/shard_map/all_gather | solution.py:11
  61.6 2.3 %reduce_sum.41 = bf16[384,768]{1,0:T(8,128)(2,1)S(1)} reduce(bf16[4,384,768]{2,1,0:T(8,128)(2,1)} %bitcast.17, bf16[]{:T(256)} %constant.53.clone.1), dimensions={0}, to_apply=%region_1.2 | reduce | flops 884736 | bytes 2949122 | tf_op jit(solution)/shard_map/reduce_sum | solution.py:11
  64.0 0.2 broadcast_in_dim.4
  64.1 1.5 %convolution_multiply_fusion.1 = f32[384,768]{1,0:T(8,128)} fusion(bf16[384,384]{1,0:T(8,128)(2,1)S(1)} %reduce_sum.40, bf16[384,768]{1,0:T(8,128)(2,1)S(1)} %reduce_sum.41, f32[48,8,6,128]{3,2,1,0:T(8,128)S(1)} %bitcast.16), kind=kOutput, calls=%fused_computation.1 | convolution fusion | flops 226787328 | bytes 3244032 | tf_op jit(solution)/shard_map/dot_general | solution.py:42
  65.6 0.0 copy-start.3
  65.6 0.0 reduce-scatter.3.cloned.1.call-update
  65.6 0.0 reduce-scatter.5.cloned.1.call-start
  65.7 0.6 copy-done.3
  66.3 23.9 %reduce-scatter.3.cloned.1.call-done = f32[96,768]{1,0:T(8,128)} async-done(((f32[384,768]{1,0:T(8,128)}), f32[96,768]{1,0:T(8,128)}) %reduce-scatter.3.cloned.1.call-update) | async-done | bytes 294928 | tf_op jit(solution)/shard_map/reduce_scatter | solution.py:46
  90.2 1.0 convert_element_type.7
  91.1 7.0 %all_gather.27 = bf16[384,768]{1,0:T(8,128)(2,1)S(1)} all-gather(bf16[96,768]{1,0:T(8,128)(2,1)S(1)} %convert_element_type.7), channel_id=1, replica_groups=mesh['row'=4,'col'=2,'rep'=4] {'rep'}, dimensions={0}, use_global_device_ids=true | all-gather | bytes 737280 | tf_op jit(solution)/shard_map/all_gather | solution.py:47
  98.1 0.1 dynamic-slice_select_fusion
  98.2 9.9 %all-gather.2 = bf16[768,384]{1,0:T(8,128)(2,1)S(1)} all-gather(bf16[384,384]{1,0:T(8,128)(2,1)S(1)} %dynamic-slice_select_fusion), channel_id=4, replica_groups=mesh['row'=4,'col'=2,'rep'=4] {'col'}, dimensions={0}, use_global_device_ids=true | all-gather | bytes 884736 | tf_op jit(solution)/shard_map/all_gather | solution.py:11
  108.1 0.2 reduce_sum.42
  108.3 0.2 broadcast_in_dim.5
  108.4 1.5 %convolution_multiply_fusion = f32[384,768]{1,0:T(8,128)} fusion(bf16[384,384]{1,0:T(8,128)(2,1)S(1)} %reduce_sum.42, bf16[384,768]{1,0:T(8,128)(2,1)S(1)} %reduce_sum.41, f32[48,8,6,128]{3,2,1,0:T(8,128)S(1)} %bitcast.15), kind=kOutput, calls=%fused_computation | convolution fusion | flops 226787328 | bytes 3244032 | tf_op jit(solution)/shard_map/dot_general | solution.py:51
  109.9 0.0 copy-start.1
  109.9 0.0 reduce-scatter.5.cloned.1.call-update
  110.0 26.3 %reduce-scatter.5.cloned.1.call-done = f32[96,768]{1,0:T(8,128)} async-done(((f32[384,768]{1,0:T(8,128)}), f32[96,768]{1,0:T(8,128)}) %reduce-scatter.5.cloned.1.call-update) | async-done | bytes 294928 | tf_op jit(solution)/shard_map/reduce_scatter | solution.py:55
  136.3 0.0 copy-done.1
  136.3 1.7 %multiply_subtract_fusion = f32[96,768]{1,0:T(8,128)} fusion(f32[96,768]{1,0:T(8,128)} %reduce-scatter.5.cloned.1.call-done, f32[96,768]{1,0:T(8,128)S(1)} %copy-done.1), kind=kLoop, calls=%fused_computation.3 | loop fusion | flops 221184 | bytes 884736 | tf_op jit(solution)/shard_map/sub | solution.py:56
  (2 shorter events, 0.0 us)
Async XLA Ops:
  6.5 2.2 %copy-start = (bf16[384,768]{1,0:T(8,128)(2,1)S(1)}, bf16[384,768]{1,0:T(8,128)(2,1)}, u32[]{:S(2)}) copy-start(bf16[384,768]{1,0:T(8,128)(2,1)} %param.3) | copy-start | bytes 1769476
  6.5 2.1 %copy-start.2 = (s32[3,6]{1,0:T(4,128)S(1)}, s32[3,6]{1,0:T(4,128)}, u32[]{:S(2)}) copy-start(s32[3,6]{1,0:T(4,128)} %param.4) | copy-start | bytes 220
  6.5 55.1 %all-gather.5.cloned.1.call-start = ((), (), s32[]{:S(2)}) async-start(), calls=%async_computation.4 | async-start | bytes 2949120 | tf_op jit(solution)/shard_map/all_gather | solution.py:11
  8.6 81.6 %reduce-scatter.3.cloned.1.call-start = ((), (), s32[]{:S(2)}) async-start(), calls=%async_computation.2 | async-start | bytes 1474560 | tf_op jit(solution)/shard_map/reduce_scatter | solution.py:46
  65.6 0.7 copy-start.3
  65.6 70.6 %reduce-scatter.5.cloned.1.call-start = ((), (), s32[]{:S(2)}) async-start(), calls=%async_computation.3 | async-start | bytes 1474560 | tf_op jit(solution)/shard_map/reduce_scatter | solution.py:55
  109.9 26.3 %copy-start.1 = (f32[96,768]{1,0:T(8,128)S(1)}, f32[96,768]{1,0:T(8,128)}, u32[]{:S(2)}) copy-start(f32[96,768]{1,0:T(8,128)} %reduce-scatter.3.cloned.1.call-done) | copy-start | bytes 884740
Sparse Core Ops, SparseCore 0:
  8.9 52.6 all-gather.4
  65.8 24.3 reduce-scatter.2
  110.1 26.1 reduce-scatter.4
